TPU v7x, 32 devices: a whole 2x2x4 slice. The times are simulated.
32 devices in a mesh: groups: 2 (over x), label: 8 (over z, y), cent: 2 (over core).
Axes of the slice: x: 2, y: 2, z: 4, core: 2. Of those that a mesh axis runs over, the one named last changes fastest.
Arguments:
- embeddings: bfloat16 [768, 16384], P('label', 'groups'), parts along dimension 1, may hold values from -40 to 40
- centroids: bfloat16 [2, 8192, 768], P('cent', ('groups', 'label')), parts along dimension 1, may hold values from -1 to 1
Outputs:
- new_centroids: float32 [2, 8192, 768], P('cent', ('groups', 'label')), parts along dimension 1
There are 2 independent parts, one for each index of `groups`. A program takes and returns all parts, laid end to end along the dimension named above; each array names one. Nothing has to cross between parts.
All inputs are finite; a program needn't handle non-finite values.
Results may differ from a plain program's by a relative error of at most 0.012.
Values may be sent and summed in bfloat16 or wider, within the bound.
A program may use at most 128 MiB of HBM per device.

v0:
```python
import jax
import jax.numpy as jnp
from jax import lax
from jax.sharding import PartitionSpec as P

prior_weight = 1.0


def weights_cent(scores):
    row_top = lax.pmax(jnp.max(scores, axis=1), "cent")
    exponent = jnp.exp(scores - row_top[:, None])
    row_sum = lax.psum(jnp.sum(exponent, axis=1), "cent")
    return (exponent / row_sum[:, None]).astype(jnp.bfloat16)


def score_against(feature_table, centroid_slice):
    half_norms = 0.5 * jnp.sum(jnp.square(centroid_slice.astype(jnp.float32)), axis=1)
    products = lax.dot_general(
        feature_table, centroid_slice, (((0,), (1,)), ((), ())), preferred_element_type=jnp.float32
    )
    return products - half_norms[None, :]


def weighted_sums(weights, feature_table):
    partial_terms = lax.dot_general(
        weights, feature_table, (((0,), (1,)), ((), ())), preferred_element_type=jnp.float32
    )
    counts = jnp.sum(weights, axis=0, dtype=jnp.float32)
    return (partial_terms, counts)


def body(embeddings, centroids):
    held_centroids = centroids[0]
    relaid = lax.all_to_all(embeddings, "label", split_axis=1, concat_axis=0, tiled=True)
    scores = score_against(relaid, lax.all_gather(centroids, "label", axis=1, tiled=True)[0])
    weights = weights_cent(scores)
    partial_terms, counts = weighted_sums(weights, relaid)
    numerators, totals = (
        lax.psum_scatter(
            partial_terms.astype(jnp.bfloat16), "label", scatter_dimension=0, tiled=True
        ).astype(jnp.float32),
        lax.psum_scatter(
            counts.astype(jnp.bfloat16), "label", scatter_dimension=0, tiled=True
        ).astype(jnp.float32),
    )
    updated = (numerators + prior_weight * held_centroids.astype(jnp.float32)) / (
        totals + prior_weight
    )[:, None]
    return updated[None]


def solution(mesh):
    return jax.shard_map(
        body,
        mesh=mesh,
        in_specs=(P("label", "groups"), P("cent", ("groups", "label"), None)),
        out_specs=P("cent", ("groups", "label"), None),
        check_vma=False,
    )
```

profile of v0, /device:TPU:0, one launch (start us, length us, event | category | flops | bytes accessed | tf_op | source)
XLA Modules:
  0.0 312.0 jit_solution(1574253930327543209)
XLA Ops:
  6.5 0.0 all-gather.2.cloned.1.call-start
  6.5 0.7 all-gather.2.cloned.1.call-update
  7.3 2.7 copy.7
  10.0 7.3 %all-to-all-start = ((bf16[96,8,1024]{2,0,1:T(8,128)(2,1)}), bf16[96,8,1024]{2,0,1:T(8,128)(2,1)S(1)}, u32[]{:S(2)}, u32[]{:S(2)}) async-start(bf16[96,8,1024]{2,0,1:T(8,128)(2,1)} %bitcast.21), calls=%async_computation | async-start | bytes 3145728 | tf_op jit(solution)/shard_map/all_to_all | solution.py:34
  17.3 0.0 reduce-scatter.2.cloned.1.call-start
  17.3 121.1 %all-gather.2.cloned.1.call-done = bf16[1,4096,768]{2,1,0:T(8,128)(2,1)} async-done(((bf16[1,512,768]{2,1,0:T(8,128)(2,1)}), bf16[1,4096,768]{2,1,0:T(8,128)(2,1)}) %all-gather.2.cloned.1.call-update) | async-done | bytes 6291472 | tf_op jit(solution)/shard_map/all_gather | solution.py:35
  138.4 4.1 %multiply_reduce_fusion = f32[4096]{0:T(1024)S(1)} fusion(bf16[1,4096,768]{2,1,0:T(8,128)(2,1)} %all-gather.2.cloned.1.call-done), kind=kLoop, calls=%fused_computation.4 | loop fusion | flops 9433088 | bytes 6307840 | tf_op jit(solution)/shard_map/reduce_sum | solution.py:17
  142.5 0.0 all-to-all-done
  142.6 13.1 %subtract_reduce_fusion = (f32[1024]{0:T(1024)S(1)}, f32[1024,4096]{1,0:T(8,128)}) fusion(f32[4096]{0:T(1024)S(1)} %broadcast_multiply_fusion, bf16[768,1024]{1,0:T(8,128)(2,1)S(1)} %bitcast.23, bf16[1,4096,768]{2,1,0:T(8,128)(2,1)} %all-gather.2.cloned.1.call-done), kind=kOutput, calls=%fused_computation.2 | convolution fusion | flops 6450838528 | bytes 24662016 | tf_op jit(solution)/shard_map/dot_general | solution.py:18
  155.6 2.4 pmax.7
  158.1 8.6 %fusion = f32[1024]{0:T(1024)S(1)} fusion(f32[1024,4096]{1,0:T(8,128)} %get-tuple-element.8, f32[1024]{0:T(1024)S(1)} %pmax.7, f32[4096]{0:T(1024)S(1)} %broadcast_multiply_fusion), kind=kLoop, calls=%fused_computation.3 | loop fusion | flops 12581888 | bytes 16801792 | tf_op jit(solution)/shard_map/reduce_sum | solution.py:12
  166.7 2.5 psum.7
  169.2 8.1 %fusion.5 = (bf16[4096]{0:T(1024)(128)(2,1)S(1)}, bf16[1024,4096]{1,0:T(8,128)(2,1)S(1)}) fusion(f32[1024]{0:T(1024)S(1)} %psum.7, f32[1024]{0:T(1024)S(1)} %pmax.7, f32[1024,4096]{1,0:T(8,128)} %get-tuple-element.8, f32[4096]{0:T(1024)S(1)} %broadcast_multiply_fusion), kind=kLoop, calls=%fused_computation.14 | loop fusion | flops 20967424 | bytes 25198592 | tf_op jit(solution)/shard_map/reduce_sum | solution.py:28
  177.2 0.0 copy-start.1
  177.3 0.0 copy-start
  177.3 9.0 %convolution_convert_fusion = bf16[4096,768]{1,0:T(8,128)(2,1)} fusion(bf16[1024,4096]{1,0:T(8,128)(2,1)S(1)} %get-tuple-element.6, bf16[768,1024]{1,0:T(8,128)(2,1)S(1)} %bitcast.24), kind=kOutput, calls=%fused_computation.5 | convolution fusion | flops 6445596672 | bytes 16252928 | tf_op jit(solution)/shard_map/dot_general | solution.py:25
  186.2 0.0 reduce-scatter.2.cloned.1.call-update
  186.3 0.0 copy-done.1
  186.3 0.6 dynamic-slice
  187.5 19.7 %all-reduce = bf16[4096]{0:T(1024)(128)(2,1)S(1)} all-reduce(bf16[4096]{0:T(1024)(128)(2,1)S(1)} %get-tuple-element.5), channel_id=3, replica_groups=mesh['groups'=2,'label'=8,'cent'=2] {'label'}, use_global_device_ids=true, to_apply=%region_7.0.clone | all-reduce | flops 4096 | bytes 16384
  207.3 0.1 convert_add_fusion.1
  207.3 95.3 %reduce-scatter.2.cloned.1.call-done = bf16[512,768]{1,0:T(8,128)(2,1)} async-done(((bf16[4096,768]{1,0:T(8,128)(2,1)}), bf16[512,768]{1,0:T(8,128)(2,1)}) %reduce-scatter.2.cloned.1.call-update) | async-done | bytes 786448 | tf_op jit(solution)/shard_map/reduce_scatter | solution.py:39
  302.6 0.0 copy-done
  302.6 2.5 fusion.4
  (1 shorter events, 0.0 us)
Async XLA Ops:
  6.5 131.9 %all-gather.2.cloned.1.call-start = ((), (), s32[]{:S(2)}) async-start(), calls=%async_computation.2 | async-start | bytes 7077888 | tf_op jit(solution)/shard_map/all_gather | solution.py:35
  10.0 132.6 %all-to-all-start = ((bf16[96,8,1024]{2,0,1:T(8,128)(2,1)}), bf16[96,8,1024]{2,0,1:T(8,128)(2,1)S(1)}, u32[]{:S(2)}, u32[]{:S(2)}) async-start(bf16[96,8,1024]{2,0,1:T(8,128)(2,1)} %bitcast.21), calls=%async_computation | async-start | bytes 3145728 | tf_op jit(solution)/shard_map/all_to_all | solution.py:34
  17.3 285.4 %reduce-scatter.2.cloned.1.call-start = ((), (), s32[]{:S(2)}) async-start(), calls=%async_computation.3 | async-start | bytes 7077888 | tf_op jit(solution)/shard_map/reduce_scatter | solution.py:39
  177.2 9.0 %copy-start.1 = (u32[32]{0:T(128)S(1)}, u32[32]{0:T(128)}, u32[]{:S(2)}) copy-start(u32[32]{0:T(128)} %constant.13) | copy-start | bytes 388
  177.3 125.4 %copy-start = (bf16[1,512,768]{2,1,0:T(8,128)(2,1)S(1)}, bf16[1,512,768]{2,1,0:T(8,128)(2,1)}, u32[]{:S(2)}) copy-start(bf16[1,512,768]{2,1,0:T(8,128)(2,1)} %param.3) | copy-start | bytes 2359300
Sparse Core Ops, SparseCore 0:
  9.5 128.8 all-gather.1
  186.4 116.2 reduce-scatter.1
where the time goes:
time: 312 us
  waiting for transfers between devices  217 us (70%)
  blocking collectives  24.6 us (8%)
  other arithmetic  23.4 us (8%)
  matrix products  22 us (7%)
  between operations  14.1 us (5%)
  starting transfers between devices  7.32 us (2%)
  local copies, waits for them, and re-layouts  3.31 us (1%)
    all_gather x1, waiting for transfers between devices, body(): lax.all_gather(centroids, 'label', axis=1, tiled=True)[0]  121 us
    reduce_scatter x1, waiting for transfers between devices, body(): lax.psum_scatter(partial_terms.astype(jnp.bfloat16), 'label', scatter_dim...  95.3 us
    unnamed x1, blocking collectives  19.7 us
    dot_general x1, matrix products, score_against(): lax.dot_general(feature_table, centroid_slice, (((0,), (1,)), ((), ())),...  13.1 us
    dot_general x1, matrix products, weighted_sums(): lax.dot_general(weights, feature_table, (((0,), (1,)), ((), ())), preferr...  8.97 us
    reduce_sum x1, other arithmetic, weights_cent(): row_sum = lax.psum(jnp.sum(exponent, axis=1), 'cent')  8.64 us
    reduce_sum x1, other arithmetic, weighted_sums(): counts = jnp.sum(weights, axis=0, dtype=jnp.float32)  8.07 us
    all_to_all x1, starting transfers between devices, body(): lax.all_to_all(embeddings, 'label', split_axis=1, concat_axis=0, tiled=True)  7.28 us
  transfers between devices with their start and end apart: 3, of which 2 were waited for; matrix products, arithmetic and copies ran while one was open for 2% of the time, Pallas kernels for 0%

commit v1 on v0

--- a/solution.py
+++ b/solution.py
@@ -1,9 +1,32 @@
+import functools
 import jax
 import jax.numpy as jnp
 from jax import lax
 from jax.sharding import PartitionSpec as P
+from jax.lax import axis_index, axis_size, ppermute
 
 prior_weight = 1.0
+
+
+def convert_sources_all(state, shard_axis):
+    val, wide_out = (axis_size(shard_axis), axis_index(shard_axis))
+    x_new = state.shape[1] // val
+    long_array = list(state.shape)
+    long_array[1] = x_new
+    lower = long_array[0]
+    long_array[0] = lower * val
+    opened = jnp.zeros(long_array, state.dtype)
+    nth = 0
+    while nth < val:
+        arr_out = lax.dynamic_slice_in_dim(state, (wide_out ^ nth) * x_new, x_new, axis=1)
+        if nth:
+            arr_out = ppermute(arr_out, shard_axis, [(dev_j, dev_j ^ nth) for dev_j in range(val)])
+        opened = lax.dynamic_update_slice_in_dim(opened, arr_out, (wide_out ^ nth) * lower, axis=0)
+        nth = nth + 1
+    return opened
+
+
+solve_the_marks = functools.partial(convert_sources_all, shard_axis="label")
 
 
 def weights_cent(scores):
@@ -31,7 +54,7 @@
 
 def body(embeddings, centroids):
     held_centroids = centroids[0]
-    relaid = lax.all_to_all(embeddings, "label", split_axis=1, concat_axis=0, tiled=True)
+    relaid = solve_the_marks(embeddings)
     scores = score_against(relaid, lax.all_gather(centroids, "label", axis=1, tiled=True)[0])
     weights = weights_cent(scores)
     partial_terms, counts = weighted_sums(weights, relaid)

time: 312 us -> 310 us (level)
  starting transfers between devices: 7.32 us -> 12.5 us
  waiting for transfers between devices: 217 us -> 213 us
    all_gather x1, waiting for transfers between devices: 121 us -> 81.2 us  [body(): lax.all_gather(centroids, 'label', axis=1, tiled=True)[0]]
    ppermute x0 -> x7, waiting for transfers between devices: none -> 35.9 us  [convert_sources_all(): ppermute(arr_out, shard_axis, [(dev_j, dev_j ^ nth) for dev_j in range(va...]
    ppermute x0 -> x7, starting transfers between devices: none -> 12.4 us  [convert_sources_all(): ppermute(arr_out, shard_axis, [(dev_j, dev_j ^ nth) for dev_j in range(va...]
    all_to_all x1 -> x0, starting transfers between devices: 7.28 us -> none  [body(): lax.all_to_all(embeddings, 'label', split_axis=1, concat_axis=0, tiled=True)]
  transfers between devices with their start and end apart: 3 -> 9, of which waited for: 2 -> 6; matrix products, arithmetic and copies ran while one was open for 2% -> 1% of each run, Pallas kernels for 0% -> 0%
where the time goes in v1:
time: 310 us
  waiting for transfers between devices  213 us (69%)
  blocking collectives  24.7 us (8%)
  other arithmetic  23.5 us (8%)
  matrix products  19.2 us (6%)
  between operations  14.2 us (5%)
  starting transfers between devices  12.5 us (4%)
  local copies, waits for them, and re-layouts  3.23 us (1%)
    reduce_scatter x1, waiting for transfers between devices, body(): lax.psum_scatter(partial_terms.astype(jnp.bfloat16), 'label', scatter_dim...  94.8 us
    all_gather x1, waiting for transfers between devices, body(): lax.all_gather(centroids, 'label', axis=1, tiled=True)[0]  81.2 us
    ppermute x7, waiting for transfers between devices, convert_sources_all(): ppermute(arr_out, shard_axis, [(dev_j, dev_j ^ nth) for dev_j in range(va...  35.9 us
    unnamed x1, blocking collectives  19.8 us
    ppermute x7, starting transfers between devices, convert_sources_all(): ppermute(arr_out, shard_axis, [(dev_j, dev_j ^ nth) for dev_j in range(va...  12.4 us
    dot_general x1, matrix products, score_against(): lax.dot_general(feature_table, centroid_slice, (((0,), (1,)), ((), ())),...  10.2 us
    dot_general x1, matrix products, weighted_sums(): lax.dot_general(weights, feature_table, (((0,), (1,)), ((), ())), preferr...  8.97 us
    reduce_sum x1, other arithmetic, weights_cent(): row_sum = lax.psum(jnp.sum(exponent, axis=1), 'cent')  8.64 us
  transfers between devices with their start and end apart: 9, of which 6 were waited for; matrix products, arithmetic and copies ran while one was open for 1% of the time, Pallas kernels for 0%

profile of v1, /device:TPU:0, one launch (start us, length us, event | category | flops | bytes accessed | tf_op | source)
XLA Modules:
  0.0 309.9 jit_solution(10795879948002125877)
XLA Ops:
  6.5 0.0 copy-start.2
  6.5 0.0 all-gather.2.cloned.1.call-start
  6.5 0.7 all-gather.2.cloned.1.call-update
  7.3 0.0 reduce-scatter.2.cloned.1.call-start
  7.3 0.2 broadcast_in_dim.4
  7.5 0.4 copy-done.2
  7.9 1.0 constant_dynamic-slice_fusion
  8.9 3.0 collective-permute-start
  11.9 1.6 collective-permute-start.1
  13.5 0.0 collective-permute-start.2
  13.5 3.0 collective-permute-start.3
  16.4 1.3 collective-permute-start.4
  17.7 0.0 collective-permute-done
  17.7 3.6 %collective-permute-start.5 = (bf16[96,1024]{1,0:T(8,128)(2,1)S(1)}, bf16[96,1024]{1,0:T(8,128)(2,1)S(1)}, u32[]{:S(2)}, u32[]{:S(2)}) collective-permute-start(bf16[96,1024]{1,0:T(8,128)(2,1)S(1)} %get-tuple-element.14), channel_id=1, source_target_pairs={{0,12},{2,14},{4,8},{6,10},{8,4},{10,6},{12,0},{14,2},{1,13},{3,15... | collective-permute-start | bytes 589832 | tf_op jit(solution)/shard_map/ppermute | solution.py:23
  21.4 10.2 %collective-permute-done.1 = bf16[96,1024]{1,0:T(8,128)(2,1)S(1)} collective-permute-done((bf16[96,1024]{1,0:T(8,128)(2,1)}, bf16[96,1024]{1,0:T(8,128)(2,1)S(1)}, u32[]{:S(2)}, u32[]{:S(2)}) %collective-permute-start.1) | collective-permute-done | bytes 196640 | tf_op jit(solution)/shard_map/ppermute | solution.py:23
  31.5 0.0 collective-permute-start.6
  31.6 4.5 %collective-permute-done.2 = bf16[96,1024]{1,0:T(8,128)(2,1)S(1)} collective-permute-done((bf16[96,1024]{1,0:T(8,128)(2,1)}, bf16[96,1024]{1,0:T(8,128)(2,1)S(1)}, u32[]{:S(2)}, u32[]{:S(2)}) %collective-permute-start.2) | collective-permute-done | bytes 196640 | tf_op jit(solution)/shard_map/ppermute | solution.py:23
  36.1 0.0 collective-permute-done.3
  36.1 18.4 %collective-permute-done.4 = bf16[96,1024]{1,0:T(8,128)(2,1)S(1)} collective-permute-done((bf16[96,1024]{1,0:T(8,128)(2,1)}, bf16[96,1024]{1,0:T(8,128)(2,1)S(1)}, u32[]{:S(2)}, u32[]{:S(2)}) %collective-permute-start.4) | collective-permute-done | bytes 196640 | tf_op jit(solution)/shard_map/ppermute | solution.py:23
  54.5 0.0 collective-permute-done.5
  54.5 2.8 collective-permute-done.6
  57.4 81.2 %all-gather.2.cloned.1.call-done = bf16[1,4096,768]{2,1,0:T(8,128)(2,1)} async-done(((bf16[1,512,768]{2,1,0:T(8,128)(2,1)}), bf16[1,4096,768]{2,1,0:T(8,128)(2,1)}) %all-gather.2.cloned.1.call-update) | async-done | bytes 6291472 | tf_op jit(solution)/shard_map/all_gather | solution.py:58
  138.5 0.0 copy-start
  138.5 4.2 %multiply_reduce_fusion = f32[4096]{0:T(1024)S(1)} fusion(bf16[1,4096,768]{2,1,0:T(8,128)(2,1)} %all-gather.2.cloned.1.call-done), kind=kLoop, calls=%fused_computation.4 | loop fusion | flops 9433088 | bytes 6307840 | tf_op jit(solution)/shard_map/reduce_sum | solution.py:40
  142.8 0.3 copy-done
  143.1 10.2 %subtract_reduce_fusion = (f32[1024]{0:T(1024)S(1)}, f32[1024,4096]{1,0:T(8,128)}) fusion(f32[4096]{0:T(1024)S(1)} %broadcast_multiply_fusion, bf16[768,1024]{1,0:T(8,128)(2,1)S(1)} %constant_dynamic-update-slice_fusion.6, bf16[1,4096,768]{2,1,0:T(8,128)(2,1)S(1)} %copy-done), kind=kOutput, calls=%fused_computation.2 | convolution fusion | flops 6450838528 | bytes 24662016 | tf_op jit(solution)/shard_map/dot_general | solution.py:41
  153.4 2.4 pmax.7
  155.8 8.6 %fusion = f32[1024]{0:T(1024)S(1)} fusion(f32[1024,4096]{1,0:T(8,128)} %get-tuple-element.16, f32[1024]{0:T(1024)S(1)} %pmax.7, f32[4096]{0:T(1024)S(1)} %broadcast_multiply_fusion), kind=kLoop, calls=%fused_computation.3 | loop fusion | flops 12581888 | bytes 16801792 | tf_op jit(solution)/shard_map/reduce_sum | solution.py:35
  164.5 2.5 psum.7
  166.9 8.1 %fusion.5 = (bf16[4096]{0:T(1024)(128)(2,1)S(1)}, bf16[1024,4096]{1,0:T(8,128)(2,1)S(1)}) fusion(f32[1024]{0:T(1024)S(1)} %psum.7, f32[1024]{0:T(1024)S(1)} %pmax.7, f32[1024,4096]{1,0:T(8,128)} %get-tuple-element.16, f32[4096]{0:T(1024)S(1)} %broadcast_multiply_fusion), kind=kLoop, calls=%fused_computation.28 | loop fusion | flops 20967424 | bytes 25198592 | tf_op jit(solution)/shard_map/reduce_sum | solution.py:51
  175.0 9.0 %convolution_convert_fusion = bf16[4096,768]{1,0:T(8,128)(2,1)} fusion(bf16[1024,4096]{1,0:T(8,128)(2,1)S(1)} %get-tuple-element.6, bf16[768,1024]{1,0:T(8,128)(2,1)S(1)} %constant_dynamic-update-slice_fusion.6), kind=kOutput, calls=%fused_computation.5 | convolution fusion | flops 6445596672 | bytes 16252928 | tf_op jit(solution)/shard_map/dot_general | solution.py:48
  184.0 0.0 copy-start.3
  184.0 0.0 copy-start.1
  184.0 0.0 reduce-scatter.2.cloned.1.call-update
  184.0 0.6 copy-done.3
  184.6 0.6 dynamic-slice
  185.9 19.8 %all-reduce = bf16[4096]{0:T(1024)(128)(2,1)S(1)} all-reduce(bf16[4096]{0:T(1024)(128)(2,1)S(1)} %get-tuple-element.5), channel_id=3, replica_groups=mesh['groups'=2,'label'=8,'cent'=2] {'label'}, use_global_device_ids=true, to_apply=%region_7.0.clone | all-reduce | flops 4096 | bytes 16384
  205.6 0.1 convert_add_fusion.1
  205.7 94.8 %reduce-scatter.2.cloned.1.call-done = bf16[512,768]{1,0:T(8,128)(2,1)} async-done(((bf16[4096,768]{1,0:T(8,128)(2,1)}), bf16[512,768]{1,0:T(8,128)(2,1)}) %reduce-scatter.2.cloned.1.call-update) | async-done | bytes 786448 | tf_op jit(solution)/shard_map/reduce_scatter | solution.py:62
  300.5 0.0 copy-done.1
  300.5 2.5 fusion.4
  (8 shorter events, 0.1 us)
Async XLA Ops:
  6.5 1.4 copy-start.2
  6.5 132.0 %all-gather.2.cloned.1.call-start = ((), (), s32[]{:S(2)}) async-start(), calls=%async_computation.1 | async-start | bytes 7077888 | tf_op jit(solution)/shard_map/all_gather | solution.py:58
  7.3 293.3 %reduce-scatter.2.cloned.1.call-start = ((), (), s32[]{:S(2)}) async-start(), calls=%async_computation.2 | async-start | bytes 7077888 | tf_op jit(solution)/shard_map/reduce_scatter | solution.py:62
  8.9 8.8 %collective-permute-start = (bf16[96,1024]{1,0:T(8,128)(2,1)}, bf16[96,1024]{1,0:T(8,128)(2,1)S(1)}, u32[]{:S(2)}, u32[]{:S(2)}) collective-permute-start(bf16[96,1024]{1,0:T(8,128)(2,1)} %get-tuple-element.12), channel_id=1, source_target_pairs={{0,2},{2,0},{4,6},{6,4},{8,10},{10,8},{12,14},{14,12},{1,3},{3,1},... | collective-permute-start | bytes 589832 | tf_op jit(solution)/shard_map/ppermute | solution.py:23
  11.9 19.6 %collective-permute-start.1 = (bf16[96,1024]{1,0:T(8,128)(2,1)}, bf16[96,1024]{1,0:T(8,128)(2,1)S(1)}, u32[]{:S(2)}, u32[]{:S(2)}) collective-permute-start(bf16[96,1024]{1,0:T(8,128)(2,1)} %get-tuple-element.11), channel_id=1, source_target_pairs={{0,4},{2,6},{4,0},{6,2},{8,12},{10,14},{12,8},{14,10},{1,5},{3,7},... | collective-permute-start | bytes 589832 | tf_op jit(solution)/shard_map/ppermute | solution.py:23
  13.5 22.6 %collective-permute-start.2 = (bf16[96,1024]{1,0:T(8,128)(2,1)}, bf16[96,1024]{1,0:T(8,128)(2,1)S(1)}, u32[]{:S(2)}, u32[]{:S(2)}) collective-permute-start(bf16[96,1024]{1,0:T(8,128)(2,1)} %get-tuple-element.10), channel_id=1, source_target_pairs={{0,6},{2,4},{4,2},{6,0},{8,14},{10,12},{12,10},{14,8},{1,7},{3,5},... | collective-permute-start | bytes 589832 | tf_op jit(solution)/shard_map/ppermute | solution.py:23
  13.5 22.6 %collective-permute-start.3 = (bf16[96,1024]{1,0:T(8,128)(2,1)}, bf16[96,1024]{1,0:T(8,128)(2,1)S(1)}, u32[]{:S(2)}, u32[]{:S(2)}) collective-permute-start(bf16[96,1024]{1,0:T(8,128)(2,1)} %get-tuple-element.9), channel_id=1, source_target_pairs={{0,8},{2,10},{4,12},{6,14},{8,0},{10,2},{12,4},{14,6},{1,9},{3,11}... | collective-permute-start | bytes 589832 | tf_op jit(solution)/shard_map/ppermute | solution.py:23
  16.4 38.1 %collective-permute-start.4 = (bf16[96,1024]{1,0:T(8,128)(2,1)}, bf16[96,1024]{1,0:T(8,128)(2,1)S(1)}, u32[]{:S(2)}, u32[]{:S(2)}) collective-permute-start(bf16[96,1024]{1,0:T(8,128)(2,1)} %get-tuple-element.8), channel_id=1, source_target_pairs={{0,10},{2,8},{4,14},{6,12},{8,2},{10,0},{12,6},{14,4},{1,11},{3,9}... | collective-permute-start | bytes 589832 | tf_op jit(solution)/shard_map/ppermute | solution.py:23
  17.7 36.8 %collective-permute-start.5 = (bf16[96,1024]{1,0:T(8,128)(2,1)S(1)}, bf16[96,1024]{1,0:T(8,128)(2,1)S(1)}, u32[]{:S(2)}, u32[]{:S(2)}) collective-permute-start(bf16[96,1024]{1,0:T(8,128)(2,1)S(1)} %get-tuple-element.14), channel_id=1, source_target_pairs={{0,12},{2,14},{4,8},{6,10},{8,4},{10,6},{12,0},{14,2},{1,13},{3,15... | collective-permute-start | bytes 589832 | tf_op jit(solution)/shard_map/ppermute | solution.py:23
  31.5 25.8 %collective-permute-start.6 = (bf16[96,1024]{1,0:T(8,128)(2,1)S(1)}, bf16[96,1024]{1,0:T(8,128)(2,1)S(1)}, u32[]{:S(2)}, u32[]{:S(2)}) collective-permute-start(bf16[96,1024]{1,0:T(8,128)(2,1)S(1)} %get-tuple-element.7), channel_id=1, source_target_pairs={{0,14},{2,12},{4,10},{6,8},{8,6},{10,4},{12,2},{14,0},{1,15},{3,13... | collective-permute-start | bytes 589832 | tf_op jit(solution)/shard_map/ppermute | solution.py:23
  138.5 4.6 %copy-start = (bf16[1,4096,768]{2,1,0:T(8,128)(2,1)S(1)}, bf16[1,4096,768]{2,1,0:T(8,128)(2,1)}, u32[]{:S(2)}) copy-start(bf16[1,4096,768]{2,1,0:T(8,128)(2,1)} %all-gather.2.cloned.1.call-done) | copy-start | bytes 18874372
  184.0 0.7 copy-start.3
  184.0 116.6 %copy-start.1 = (bf16[1,512,768]{2,1,0:T(8,128)(2,1)S(1)}, bf16[1,512,768]{2,1,0:T(8,128)(2,1)}, u32[]{:S(2)}) copy-start(bf16[1,512,768]{2,1,0:T(8,128)(2,1)} %param.3) | copy-start | bytes 2359300
Sparse Core Ops, SparseCore 0:
  9.5 128.9 all-gather.1
  184.1 116.3 reduce-scatter.1
